TPU v7x, 32 devices: a whole 2x2x4 slice. The times are simulated.
32 devices in a mesh: segment: 4 (over y, x), tile: 8 (over z, core).
Axes of the slice: x: 2, y: 2, z: 4, core: 2. Of those that a mesh axis runs over, the one named last changes fastest.
Arguments:
- raw_frames: bfloat16 [32, 1280, 1280], P(('segment', 'tile')), may hold values from -6 to 6
- dark_frame: bfloat16 [1280, 1280], replicated, may hold values from -2.5 to 2.5
- flat_field: bfloat16 [1280, 1280], replicated, may hold values from 0.25 to 1.75
- seeing: float32 [32, 64], P(None, 'tile'), may hold values from 0.1 to 10
- anchors: int32 [64, 2], replicated, may hold values from 0 to 1023, as said below
- taper: int32 [64], replicated, may hold values from 16 to 64
Outputs:
- power: float32 [64, 256, 256], P('tile', 'segment')
- cross: float32 [64, 4, 256, 256], P('tile', None, 'segment')
Inputs may be any that keep to these rules, and one draw needn't show every extreme that they name: `anchors`: the subfield g = 8 i + j has anchor (128 i + a, 128 j + b) with a and b below 128.
All inputs are finite; a program needn't handle non-finite values.
Results may differ from a plain program's by a relative error of at most 0.013.
Values may be sent and summed in bfloat16 or wider, within the bound.
No kernel may reach another device: no remote copies, remote signals or barrier semaphores. Data moves between devices by JAX's collectives and lax.ppermute only.
A program may use at most 192 MiB of HBM per device.

v0:
```python
import math

import jax
import jax.numpy as jnp
from jax import lax
from jax.sharding import PartitionSpec as P

S = 256


def ramp_rows(taper, size):
    place = jnp.arange(size, dtype=jnp.float32)[None, :]
    width = taper.astype(jnp.float32)[:, None]
    left = jnp.where(place < width, 0.5 - 0.5 * jnp.cos(jnp.pi * (place + 0.5) / width), 1.0)
    return left * left[:, ::-1]


def dft_tables(size):
    steps = jnp.arange(size, dtype=jnp.int32)
    phase = steps[:, None] * steps[None, :] % size
    angle = 2.0 * jnp.pi * phase.astype(jnp.float32) / size
    factor = 1.0 / jnp.sqrt(jnp.float32(size))
    return (
        (jnp.cos(angle) * factor).astype(jnp.bfloat16),
        (jnp.sin(angle) * factor).astype(jnp.bfloat16),
    )


def first_pass(sub, cosine, sine):
    table = jnp.concatenate([cosine, -sine], axis=1)
    return jnp.einsum("fsxy,yk->fsxk", sub, table, preferred_element_type=jnp.float32).astype(
        jnp.bfloat16
    )


def second_pass(half, cosine, sine):
    size = cosine.shape[0]
    with_cos = jnp.einsum("ux,fsxk->fsuk", cosine, half, preferred_element_type=jnp.float32)
    with_sin = jnp.einsum("ux,fsxk->fsuk", sine, half, preferred_element_type=jnp.float32)
    real_part = with_cos[..., :size] + with_sin[..., size:]
    imag_part = with_cos[..., size:] - with_sin[..., :size]
    return (real_part, imag_part)


def local(raw_frames, dark_frame, flat_field, seeing, anchors, taper):
    size = S
    cosine, sine = dft_tables(size)
    ramps = ramp_rows(taper, size)
    calibrated = (
        raw_frames.astype(jnp.float32) - dark_frame.astype(jnp.float32)[None]
    ) / flat_field.astype(jnp.float32)[None]

    def cutout(anchor, ramp):
        start = jnp.zeros((), jnp.int32)
        cal = lax.dynamic_slice(
            calibrated, (start, anchor[0], anchor[1]), (calibrated.shape[0], size, size)
        )
        centered = cal - jnp.mean(cal, axis=(1, 2), keepdims=True)
        return (centered * (ramp[:, None] * ramp[None, :])[None]).astype(jnp.bfloat16)

    sub = jax.vmap(cutout, in_axes=(0, 0), out_axes=1)(anchors, ramps)
    received = lax.all_to_all(sub, "tile", split_axis=1, concat_axis=0, tiled=True)
    n_frames = received.shape[0]
    sub_dev = received.shape[1]
    block = math.gcd(n_frames, 8)
    n_blocks = n_frames // block
    segment_index = lax.axis_index("segment")
    weights = lax.dynamic_slice_in_dim(seeing, segment_index * n_frames, n_frames, 0)
    weight_sum = jnp.sum(seeing, axis=0)
    blocks = received.reshape((n_blocks, block) + received.shape[1:])
    weight_blocks = weights.reshape(n_blocks, block, sub_dev)

    def accumulate(carry, inputs):
        data, wblock = inputs
        half = first_pass(data, cosine, sine)
        real_part, imag_part = second_pass(half, cosine, sine)
        wgt = wblock[:, :, None, None]
        power_sum = carry[0] + jnp.sum(
            wgt * (real_part * real_part + imag_part * imag_part), axis=0
        )
        real_u = jnp.roll(real_part, -1, axis=2)
        imag_u = jnp.roll(imag_part, -1, axis=2)
        real_v = jnp.roll(real_part, -1, axis=3)
        imag_v = jnp.roll(imag_part, -1, axis=3)
        cross_sum = carry[1] + jnp.stack(
            [
                jnp.sum(wgt * (real_part * real_u + imag_part * imag_u), axis=0),
                jnp.sum(wgt * (imag_part * real_u - real_part * imag_u), axis=0),
                jnp.sum(wgt * (real_part * real_v + imag_part * imag_v), axis=0),
                jnp.sum(wgt * (imag_part * real_v - real_part * imag_v), axis=0),
            ],
            axis=1,
        )
        return ((power_sum, cross_sum), None)

    start_power = jnp.zeros((sub_dev, size, size), jnp.float32)
    start_cross = jnp.zeros((sub_dev, 4, size, size), jnp.float32)
    (power_sum, cross_sum), unused = lax.scan(
        accumulate, (start_power, start_cross), (blocks, weight_blocks)
    )
    power_rows, cross_rows = (
        lax.psum_scatter(
            power_sum.astype(jnp.bfloat16), "segment", scatter_dimension=1, tiled=True
        ).astype(jnp.float32),
        lax.psum_scatter(
            cross_sum.astype(jnp.bfloat16), "segment", scatter_dimension=2, tiled=True
        ).astype(jnp.float32),
    )
    power = power_rows / weight_sum[:, None, None]
    cross = cross_rows / weight_sum[:, None, None, None]
    return (power, cross)


def solution(mesh):
    placed = (P(("segment", "tile"), None, None), P(), P(), P(None, "tile"), P(), P())
    return jax.shard_map(
        local,
        mesh=mesh,
        in_specs=placed,
        out_specs=(P("tile", "segment", None), P("tile", None, "segment", None)),
        check_vma=False,
    )
```

profile of v0, /device:TPU:0, one launch (start us, length us, event | category | flops | bytes accessed | tf_op | source)
XLA Modules:
  0.0 745.8 jit_solution(13757384058877534190)
XLA Ops:
  9.4 7.9 %convert_divide_fusion = f32[1,1280,1280]{2,1,0:T(8,128)} fusion(bf16[1,1280,1280]{2,1,0:T(8,128)(2,1)} %param.6, bf16[1280,1280]{1,0:T(8,128)(2,1)} %param.8, bf16[1280,1280]{1,0:T(8,128)(2,1)} %param.7), kind=kLoop, calls=%fused_computation.19 | loop fusion | flops 8192000 | bytes 16384000 | tf_op jit(solution)/shard_map/div | solution.py:49
  17.3 242.0 %while.1 = (s32[]{:T(128)}, f32[1,1280,1280]{2,1,0:T(8,128)}, s32[64,3]{0,1:T(4,128)S(1)}, f32[64,1,256,256]{3,2,1,0:T(8,128)}, s32[]{:T(128)}) while((s32[]{:T(128)}, f32[1,1280,1280]{2,1,0:T(8,128)}, s32[64,3]{0,1:T(4,128)S(1)}, f32[64,1,256,256]{3,2,1,0:T(8,128)}, s32[]{:T(128)}) %tuple.34), condition=%wide.while_cond, body=%wide.while_body.sunk | while | flops 2 | bytes 525929 | solution.py:55
  33.1 3.1 bitcast_dynamic-update-slice_fusion.2
  48.2 3.1 bitcast_dynamic-update-slice_fusion.2
  63.3 3.1 bitcast_dynamic-update-slice_fusion.2
  89.8 3.1 bitcast_dynamic-update-slice_fusion.2
  97.4 3.1 bitcast_dynamic-update-slice_fusion.2
  135.2 3.1 bitcast_dynamic-update-slice_fusion.2
  146.5 3.1 bitcast_dynamic-update-slice_fusion.2
  150.3 3.1 bitcast_dynamic-update-slice_fusion.2
  157.9 3.1 bitcast_dynamic-update-slice_fusion.2
  169.3 3.1 bitcast_dynamic-update-slice_fusion.2
  207.1 3.1 bitcast_dynamic-update-slice_fusion.2
  259.3 7.0 reduce_sum.68
  266.3 9.7 %fusion.1 = bf16[1,64,256,256]{3,2,0,1:T(8,128)(2,1)} fusion(f32[64,1,256,256]{3,2,1,0:T(8,128)} %get-tuple-element.30, f32[64,256]{1,0:T(8,128)S(1)} %fusion.16, f32[64]{0:T(128)S(1)} %broadcast_multiply_fusion), kind=kLoop, calls=%fused_computation.10 | loop fusion | flops 16777216 | bytes 25231616 | tf_op jit(solution)/shard_map/vmap()/convert_element_type | solution.py:59
  276.0 6.4 all-to-all-start
  284.5 181.8 %all-to-all-done = bf16[1,64,256,256]{3,2,0,1:T(8,128)(2,1)} async-done(((bf16[1,64,256,256]{3,2,0,1:T(8,128)(2,1)}), bf16[1,64,256,256]{3,2,0,1:T(8,128)(2,1)}, u32[]{:S(2)}, u32[]{:S(2)}) %all-to-all-start) | async-done | bytes 8388640 | tf_op jit(solution)/shard_map/all_to_all | solution.py:62
  466.3 11.6 %convolution_convert_fusion = bf16[8,8,256,512]{3,2,1,0:T(8,128)(2,1)} fusion(bf16[8,8,256,256]{3,2,1,0:T(8,128)(2,1)} %bitcast.3, bf16[256,256]{1,0:T(8,128)(2,1)S(1)} %fusion.12, bf16[256,256]{1,0:T(8,128)(2,1)S(1)} %multiply_convert_fusion.1), kind=kOutput, calls=%fused_computation.18 | convolution fusion | flops 4303880192 | bytes 25427968 | tf_op jit(solution)/shard_map/while/body/eval_jaxpr/fsxy,yk->fsxk/dot_general | solution.py:31
  477.9 22.3 %convolution_bitcast_fusion = f32[8,8,256,512]{2,3,1,0:T(8,128)} fusion(bf16[8,8,256,512]{3,2,1,0:T(8,128)(2,1)} %convolution_convert_fusion), kind=kOutput, calls=%fused_computation.16 | convolution fusion | flops 4296015872 | bytes 50331648 | tf_op jit(solution)/shard_map/while/body/eval_jaxpr/ux,fsxk->fsuk/dot_general | solution.py:39
  500.3 22.3 %convolution_bitcast_fusion.1 = f32[8,8,256,512]{2,3,1,0:T(8,128)} fusion(bf16[8,8,256,512]{3,2,1,0:T(8,128)(2,1)} %convolution_convert_fusion), kind=kOutput, calls=%fused_computation.17 | convolution fusion | flops 4296015872 | bytes 50331648 | tf_op jit(solution)/shard_map/while/body/eval_jaxpr/ux,fsxk->fsuk/dot_general | solution.py:38
  522.6 34.0 %slice_add_fusion = (f32[8,8,256,256]{2,3,1,0:T(8,128)}, f32[8,8,256,256]{2,3,1,0:T(8,128)}) fusion(f32[8,8,256,512]{2,3,1,0:T(8,128)} %convolution_bitcast_fusion, f32[8,8,256,512]{2,3,1,0:T(8,128)} %convolution_bitcast_fusion.1), kind=kLoop, calls=%fused_computation.3 | loop fusion | flops 8388608 | bytes 100663296 | tf_op jit(solution)/shard_map/while/body/eval_jaxpr/add | solution.py:40
  556.6 15.4 %slice.91 = f32[8,8,255,256]{2,3,1,0:T(8,128)} slice(f32[8,8,256,256]{2,3,1,0:T(8,128)} %get-tuple-element.52), slice={[0:8], [0:8], [1:256], [0:256]} | slice | bytes 33423360 | tf_op jit(solution)/shard_map/while/body/eval_jaxpr/jit(_roll_static)/slice | solution.py:81
  573.1 8.5 %slice.95 = f32[8,8,256,255]{2,3,1,0:T(8,128)} slice(f32[8,8,256,256]{2,3,1,0:T(8,128)S(1)} %copy-done), slice={[0:8], [0:8], [0:256], [1:256]} | slice | bytes 33423360 | tf_op jit(solution)/shard_map/while/body/eval_jaxpr/jit(_roll_static)/slice | solution.py:83
  583.8 7.5 %slice.93 = f32[8,8,255,256]{2,3,1,0:T(8,128)} slice(f32[8,8,256,256]{2,3,1,0:T(8,128)S(1)} %bitcast.58), slice={[0:8], [0:8], [1:256], [0:256]} | slice | bytes 33423360 | tf_op jit(solution)/shard_map/while/body/eval_jaxpr/jit(_roll_static)/slice | solution.py:82
  591.3 6.5 slice.97
  597.7 4.0 slice.92
  601.7 7.7 %slice.94 = f32[8,8,1,256]{2,3,1,0:T(8,128)} slice(f32[8,8,256,256]{2,3,1,0:T(8,128)} %get-tuple-element.53), slice={[0:8], [0:8], [0:1], [0:256]} | slice | bytes 131072 | tf_op jit(solution)/shard_map/while/body/eval_jaxpr/jit(_roll_static)/slice | solution.py:82
  610.5 39.9 %multiply_reduce_fusion.3 = (bf16[8,256,256]{1,2,0:T(8,128)(2,1)S(1)}, bf16[8,256,256]{1,2,0:T(8,128)(2,1)S(1)}, bf16[8,256,256]{1,2,0:T(8,128)(2,1)}, bf16[8,256,256]{1,2,0:T(8,128)(2,1)}, bf16[8,256,256]{1,2,0:T(8,128)(2,1)S(1)}) fusion(f32[8,8,256,256]{2,3,1,0:T(8,128)} %get-tuple-element.53, f32[8,8,256,256]{2,3,1,0:T(8,128)} %get-tuple-element.52, ...), kind=kLoop, calls=%fused_computation.14 | loop fusion | flops 119013376 | bytes 105906432 | tf_op jit(solution)/shard_map/while/body/eval_jaxpr/reduce_sum | solution.py:87
  652.3 3.7 pad_maximum_fusion.4
  656.0 8.0 %copy.20 = bf16[8,4,256,256]{3,0,1,2:T(8,128)(2,1)} copy(bf16[8,4,256,256]{2,3,0,1:T(8,128)(2,1)} %pad_maximum_fusion.4) | data formatting | bytes 8388608 | tf_op jit(solution)/shard_map/while/body/eval_jaxpr/stack | solution.py:85
  664.1 15.2 %reduce-scatter.3.cloned.1.call-done = bf16[8,64,256]{2,0,1:T(8,128)(2,1)} async-done(((bf16[8,256,256]{2,0,1:T(8,128)(2,1)}), bf16[8,64,256]{2,0,1:T(8,128)(2,1)}) %reduce-scatter.3.cloned.1.call-update) | async-done | bytes 262160 | tf_op jit(solution)/shard_map/reduce_scatter | solution.py:102
  681.3 53.6 %reduce-scatter.5.cloned.1.call-done = bf16[8,4,64,256]{3,0,1,2:T(8,128)(2,1)} async-done(((bf16[8,4,256,256]{3,0,1,2:T(8,128)(2,1)}), bf16[8,4,64,256]{3,0,1,2:T(8,128)(2,1)}) %reduce-scatter.5.cloned.1.call-update) | async-done | bytes 1048592 | tf_op jit(solution)/shard_map/reduce_scatter | solution.py:105
  (222 shorter events, 224.5 us)
Async XLA Ops:
  266.3 16.1 %copy-start.1 = (f32[32,8]{0,1:T(8,128)S(1)}, f32[32,8]{0,1:T(8,128)}, u32[]{:S(2)}) copy-start(f32[32,8]{0,1:T(8,128)} %param.9) | copy-start | bytes 3076
  276.0 190.3 %all-to-all-start = ((bf16[1,64,256,256]{3,2,0,1:T(8,128)(2,1)}), bf16[1,64,256,256]{3,2,0,1:T(8,128)(2,1)}, u32[]{:S(2)}, u32[]{:S(2)}) async-start(bf16[1,64,256,256]{3,2,0,1:T(8,128)(2,1)} %fusion.1), calls=%async_computation | async-start | bytes 16777216 | tf_op jit(solution)/shard_map/all_to_all | solution.py:62
  282.3 396.9 %reduce-scatter.3.cloned.1.call-start = ((), (), s32[]{:S(2)}) async-start(), calls=%async_computation.3 | async-start | bytes 1310720 | tf_op jit(solution)/shard_map/reduce_scatter | solution.py:102
  556.6 16.5 %copy-start = (f32[8,8,256,256]{2,3,1,0:T(8,128)S(1)}, f32[8,8,256,256]{2,3,1,0:T(8,128)}, u32[]{:S(2)}) copy-start(f32[8,8,256,256]{2,3,1,0:T(8,128)} %get-tuple-element.52) | copy-start | bytes 50331652
  556.6 25.0 %slice-start = ((s8[16777216]{0:T(1024)(128)(4,1)}), s8[4194304]{0:T(1024)(128)(4,1)S(1)}, s32[]{:S(2)}) async-start(s8[16777216]{0:T(1024)(128)(4,1)} %bitcast.57), calls=%async_computation.5 | async-start | bytes 8388608
  556.6 25.0 %slice-start.1 = ((s8[16777216]{0:T(1024)(128)(4,1)}), s8[4194304]{0:T(1024)(128)(4,1)S(1)}, s32[]{:S(2)}) async-start(s8[16777216]{0:T(1024)(128)(4,1)} %bitcast.57), calls=%async_computation.6 | async-start | bytes 8388608
  573.1 9.1 %slice-start.2 = ((s8[16777216]{0:T(1024)(128)(4,1)}), s8[4194304]{0:T(1024)(128)(4,1)S(1)}, s32[]{:S(2)}) async-start(s8[16777216]{0:T(1024)(128)(4,1)} %bitcast.57), calls=%async_computation.7 | async-start | bytes 8388608
  573.1 10.7 %slice-start.3 = ((s8[16777216]{0:T(1024)(128)(4,1)}), s8[4194304]{0:T(1024)(128)(4,1)S(1)}, s32[]{:S(2)}) async-start(s8[16777216]{0:T(1024)(128)(4,1)} %bitcast.57), calls=%async_computation.8 | async-start | bytes 8388608
  650.4 13.6 %copy-start.2 = (f32[32,8]{0,1:T(8,128)S(1)}, f32[32,8]{0,1:T(8,128)}, u32[]{:S(2)}) copy-start(f32[32,8]{0,1:T(8,128)} %param.9) | copy-start | bytes 3076
  652.2 82.6 %reduce-scatter.5.cloned.1.call-start = ((), (), s32[]{:S(2)}) async-start(), calls=%async_computation.4 | async-start | bytes 5242880 | tf_op jit(solution)/shard_map/reduce_scatter | solution.py:105
Sparse Core Ops, SparseCore 0:
  652.4 26.8 reduce-scatter.2
  682.3 52.5 reduce-scatter.4
where the time goes:
time: 752 us; the launch traced here: 746 us
  local copies, waits for them, and re-layouts  309 us (41%)
  waiting for transfers between devices  251 us (33%)
  other arithmetic  109 us (14%)
  matrix products  56.3 us (7%)
  between operations  14.1 us (2%)
    gather x192, local copies, waits for them, and re-layouts  242 us
    all_to_all x1, waiting for transfers between devices, local(): lax.all_to_all(sub, 'tile', split_axis=1, concat_axis=0, tiled=True)  182 us
    reduce_scatter x1, waiting for transfers between devices, local(): lax.psum_scatter(cross_sum.astype(jnp.bfloat16), 'segment', scatter_dimen...  53.6 us
    reduce_sum x1, other arithmetic, accumulate(): jnp.sum(wgt * (real_part * real_u + imag_part * imag_u), axis=0)  39.9 us
    add x1, other arithmetic, second_pass(): real_part = with_cos[..., :size] + with_sin[..., size:]  34 us
    dot_general x1, matrix products, second_pass(): jnp.einsum('ux,fsxk->fsuk', sine, half, preferred_element_type=jnp.float32)  22.3 us
    dot_general x1, matrix products, second_pass(): jnp.einsum('ux,fsxk->fsuk', cosine, half, preferred_element_type=jnp.floa...  22.3 us
    slice x2, local copies, waits for them, and re-layouts, accumulate(): real_u = jnp.roll(real_part, -1, axis=2)  19.3 us
  transfers between devices with their start and end apart: 3, of which 3 were waited for; matrix products, arithmetic and copies ran while one was open for 2% of the time, Pallas kernels for 0%

commit v1 on v0

--- a/solution.py
+++ b/solution.py
@@ -2,10 +2,296 @@
 
 import jax
 import jax.numpy as jnp
+import numpy as np
 from jax import lax
+from jax.experimental import pallas as pl
+from jax.experimental.pallas import tpu as pltpu
 from jax.sharding import PartitionSpec as P
 
 S = 256
+HALF = 128
+WIN = 384
+ROWS = 656
+BF = jnp.bfloat16
+F32 = jnp.float32
+
+
+def ramp_at(place, width):
+    def side(x):
+        return jnp.where(x < width, 0.5 - 0.5 * jnp.cos(jnp.pi * (x + 0.5) / width), 1.0)
+
+    inside = (place >= 0) & (place < S)
+    return jnp.where(inside, side(place) * side(S - 1.0 - place), 0.0)
+
+
+def half_tables():
+    def angle(n, m):
+        return 2.0 * np.pi * ((np.arange(n)[:, None] * np.arange(m)[None, :]) % S) / S
+
+    first = angle(WIN, S)
+    second = angle(HALF + 8, S)
+    t = np.concatenate([np.cos(first), -np.sin(first)], axis=1) / 16.0
+    w = np.concatenate([np.cos(second), np.sin(second)], axis=0) / 16.0
+    return jnp.asarray(t.astype(np.float32)).astype(BF), jnp.asarray(w.astype(np.float32)).astype(BF)
+
+
+def spectra_body(n_frames, rows, wts, wa, wb, da, db, fa, fb, rx, ry, mk, t_ref, w_ref, keep, give, cal, sub, z, y):
+    k = pl.program_id(0)
+    for h, (w, d, f) in enumerate(((wa, da, fa), (wb, db, fb))):
+
+        def calibrate(step, carry, h=h, w=w, d=d, f=f):
+            at = pl.multiple_of(step * 16, 16)
+            inverse = 1.0 / f[pl.ds(at, 16), :].astype(F32)
+            dark = d[pl.ds(at, 16), :].astype(F32)
+            for fr in range(n_frames):
+                value = (w[fr, pl.ds(at, 16), :].astype(F32) - dark) * inverse
+                for n in range(4):
+                    cal[fr, n, pl.ds(h * S + at, 16), :] = value[:, n * HALF : (n + 1) * HALF]
+            return carry
+
+        lax.fori_loop(0, S // 16, calibrate, 0)
+
+    def one(q, carry):
+        which, col = q // 2, q % 2
+        start = rows[k * 4 + q]
+        rowr = ry[q, 0:1, :]
+        mask = mk[q, 0:1, :]
+        for fr in range(n_frames):
+            mean = jnp.zeros((1, 1), F32)
+            for m in range(3):
+                total = cal[fr, col + m, pl.ds(start, 8), :]
+                for n in range(1, S // 8):
+                    total = total + cal[fr, col + m, pl.ds(start + 8 * n, 8), :]
+                weighed = jnp.sum(total * mask[:, m * HALF : (m + 1) * HALF], axis=0, keepdims=True)
+                mean = mean + jnp.sum(weighed, axis=1, keepdims=True)
+            for n in range(S // 16):
+                col_r = rx[q, 16 * n : 16 * n + 16, :]
+                for m in range(3):
+                    c = cal[fr, col + m, pl.ds(start + 16 * n, 16), :]
+                    ramp = col_r * rowr[:, m * HALF : (m + 1) * HALF]
+                    sub[fr, 16 * n : 16 * n + 16, m * HALF : (m + 1) * HALF] = ((c - mean) * ramp).astype(BF)
+        for fr in range(n_frames):
+            z[fr] = jnp.dot(sub[fr], t_ref[...], preferred_element_type=F32).astype(BF)
+        for fr in range(n_frames):
+            both = jnp.dot(w_ref[...], z[fr], preferred_element_type=F32)
+            for n in range(4):
+                y[fr, n] = both[:, n * HALF : (n + 1) * HALF]
+
+        def spec_rows(fr, at, n):
+            a = [y[fr, m, pl.ds(at, n), :] for m in range(4)]
+            b = [y[fr, m, pl.ds(at + HALF + 8, n), :] for m in range(4)]
+            re = jnp.concatenate([a[0] + b[2], a[1] + b[3]], axis=1)
+            return re, jnp.concatenate([a[2] - b[0], a[3] - b[1]], axis=1)
+
+        def weighted(at, n, shift_u):
+            acc = None
+            for fr in range(n_frames):
+                wgt = wts[(k * 4 + q) * n_frames + fr]
+                re, im = spec_rows(fr, at, n)
+                wre, wim = re * wgt, im * wgt
+                re_v, im_v = pltpu.roll(re, S - 1, axis=1), pltpu.roll(im, S - 1, axis=1)
+                terms = [wre * re + wim * im]
+                if shift_u:
+                    re_u, im_u = spec_rows(fr, at + 1, n)
+                    terms += [wre * re_u + wim * im_u, wim * re_u - wre * im_u]
+                terms += [wre * re_v + wim * im_v, wim * re_v - wre * im_v]
+                acc = terms if acc is None else [p + r for p, r in zip(acc, terms)]
+            return acc
+
+        def store(at, value):
+            @pl.when(which == 0)
+            def _():
+                keep[0, col, pl.ds(at, 16), :] = value
+
+            @pl.when(which == 1)
+            def _():
+                give[0, col, pl.ds(at, 16), :] = value
+
+        def block(r, c2):
+            at = pl.multiple_of(r * 16, 16)
+            acc = weighted(at, 16, True)
+            for n, value in enumerate(acc):
+                store(pl.multiple_of(n * HALF + at, 16), value.astype(BF))
+            return c2
+
+        lax.fori_loop(0, HALF // 16, block, 0)
+        last = [jnp.broadcast_to(v[0:1, :], (16, S)) for v in weighted(HALF, 8, False)]
+        line = lax.broadcasted_iota(jnp.int32, (16, S), 0)
+        tail = jnp.where(line == 0, last[0], jnp.where(line == 1, last[1], jnp.where(line == 2, last[2], 0.0)))
+        store(5 * HALF, tail.astype(BF))
+        return carry
+
+    lax.fori_loop(0, 4, one, 0)
+
+
+def spectra(rows, wts, win, dark, flat, rx, ry, mk, t, w):
+    n_frames, height, width = win.shape
+    steps = height // S - 1
+    vm = pltpu.VMEM
+
+    def pair(shape, lead):
+        return [
+            pl.BlockSpec(shape, lambda k, r, s, d=d: (0,) * lead + (k + d, 0)) for d in (0, 1)
+        ]
+
+    def whole(shape):
+        return pl.BlockSpec(shape, lambda k, r, s: (0,) * len(shape))
+
+    def per_step(shape):
+        return pl.BlockSpec(shape, lambda k, r, s: (k,) + (0,) * (len(shape) - 1))
+
+    out = jax.ShapeDtypeStruct((steps, 2, ROWS, S), BF)
+    return pl.pallas_call(
+        lambda *refs: spectra_body(n_frames, *refs),
+        out_shape=(out, out),
+        grid_spec=pltpu.PrefetchScalarGridSpec(
+            num_scalar_prefetch=2,
+            grid=(steps,),
+            in_specs=pair((n_frames, S, width), 1)
+            + pair((S, width), 0)
+            + pair((S, width), 0)
+            + [per_step((4, S, HALF)), per_step((4, 8, WIN)), per_step((4, 8, WIN)), whole(t.shape), whole(w.shape)],
+            out_specs=(per_step((1, 2, ROWS, S)), per_step((1, 2, ROWS, S))),
+            scratch_shapes=[
+                vm((n_frames, width // HALF, 2 * S, HALF), F32),
+                vm((n_frames, S, WIN), BF),
+                vm((n_frames, S, 2 * S), BF),
+                vm((n_frames, 4, 2 * HALF + 16, HALF), F32),
+            ],
+        ),
+        compiler_params=pltpu.CompilerParams(dimension_semantics=("arbitrary",), vmem_limit_bytes=56 << 20),
+        cost_estimate=pl.CostEstimate(flops=16_000_000_000, bytes_accessed=20_000_000, transcendentals=0),
+        name="spectra",
+    )(rows, wts, win, win, dark, dark, flat, flat, rx, ry, mk, t, w)
+
+
+def finish_body(scal, x, flip, rot, lines, power, cross):
+    def moved(n, m, at):
+        right = jnp.dot(x[n, m], at, preferred_element_type=F32).astype(BF)
+        return jnp.dot(lines[...], right, preferred_element_type=F32)
+
+    n = pl.program_id(0)
+    for m in range(2):
+        g = n * 2 + m
+        inv, cb, sb = scal[g * 3], scal[g * 3 + 1], scal[g * 3 + 2]
+        got = [jnp.dot(x[0, m, p], (flip if p < 3 else rot)[...], preferred_element_type=F32).astype(BF) for p in range(5)]
+        got = [jnp.dot(lines[...], v, preferred_element_type=F32) for v in got]
+        power[m] = got[0] * inv
+        cross[m, 0] = got[1] * inv
+        cross[m, 1] = got[2] * inv
+        cross[m, 2] = (got[3] * cb + got[4] * sb) * inv
+        cross[m, 3] = (got[4] * cb - got[3] * sb) * inv
+
+
+def finish(scal, x, flip, rot, lines):
+    n_seg, per, _, height, _ = x.shape
+    count = n_seg * per
+
+    def whole(a):
+        return pl.BlockSpec(a.shape, lambda k, s: (0,) * a.ndim)
+
+    return pl.pallas_call(
+        finish_body,
+        out_shape=(
+            jax.ShapeDtypeStruct((count, height, S), F32),
+            jax.ShapeDtypeStruct((count, 4, height, S), F32),
+        ),
+        grid_spec=pltpu.PrefetchScalarGridSpec(
+            num_scalar_prefetch=1,
+            grid=(n_seg,),
+            in_specs=[
+                pl.BlockSpec((1, per, 5, height, S), lambda k, s: (k, 0, 0, 0, 0)),
+                whole(flip),
+                whole(rot),
+                whole(lines),
+            ],
+            out_specs=(
+                pl.BlockSpec((per, height, S), lambda k, s: (k, 0, 0)),
+                pl.BlockSpec((per, 4, height, S), lambda k, s: (k, 0, 0, 0)),
+            ),
+        ),
+        compiler_params=pltpu.CompilerParams(dimension_semantics=("arbitrary",)),
+        cost_estimate=pl.CostEstimate(flops=400_000_000, bytes_accessed=4_000_000, transcendentals=0),
+        name="finish",
+    )(scal, x, flip, rot, lines)
+
+
+def pick(array, index, axis):
+    return lax.dynamic_index_in_dim(array, index, axis, keepdims=False)
+
+
+def planes(raw_frames, dark_frame, flat_field, seeing, anchors, taper):
+    seg = lax.axis_index("segment")
+    tile = lax.axis_index("tile")
+    z, core = tile // 2, tile % 2
+
+    send = jnp.stack([raw_frames[0, :, S * d : S * d + 2 * S] for d in range(4)])
+    win = lax.all_to_all(send, "segment", split_axis=0, concat_axis=0, tiled=True)
+
+    by_tile = seeing.reshape(4, 8, 8).transpose(1, 0, 2)
+    weights = lax.all_to_all(by_tile, "tile", split_axis=0, concat_axis=0, tiled=True)
+
+    def mine(grid_array):
+        cols = lax.dynamic_slice_in_dim(grid_array, 2 * seg, 2, 1)
+        cols = cols.reshape((4, 2) + cols.shape[1:])
+        return jnp.where(core == 0, cols, cols[:, ::-1])
+
+    wts = mine(weights.transpose(0, 2, 1)).reshape(-1)
+    spots = anchors.reshape(8, 8, 2)
+    offset = spots - 128 * jnp.stack(jnp.meshgrid(jnp.arange(8), jnp.arange(8), indexing="ij"), -1)
+    rows = (mine(spots[..., 0]) - S * jnp.arange(4)[:, None, None]).reshape(-1)
+    shift = mine(offset[..., 1]).reshape(-1).astype(F32)
+    width = mine(taper.reshape(8, 8)).reshape(-1).astype(F32)
+    x = jnp.arange(S, dtype=F32)
+    rx = jnp.broadcast_to(ramp_at(x[None, :], width[:, None])[:, :, None], (16, S, HALF))
+    place = jnp.arange(WIN, dtype=F32)[None, :] - shift[:, None]
+    ry = jnp.broadcast_to(ramp_at(place, width[:, None])[:, None, :], (16, 8, WIN))
+    inside = jnp.where((place >= 0) & (place < S), 1.0 / (S * S), 0.0)
+    mk = jnp.broadcast_to(inside[:, None, :], (16, 8, WIN))
+    dark = lax.dynamic_slice_in_dim(dark_frame, S * seg, 2 * S, 1)
+    flat = lax.dynamic_slice_in_dim(flat_field, S * seg, 2 * S, 1)
+
+    t, w = half_tables()
+    keep, give = spectra(rows.astype(jnp.int32), wts, win, dark, flat, rx, ry, mk, t, w)
+
+    other = lax.ppermute(give, "tile", [(n, n ^ 1) for n in range(8)])
+
+    def own(index):
+        index = jnp.clip(index, 0, 3)
+        return pick(keep, index, 0).astype(F32) + pick(other, index, 0).astype(F32)
+
+    up = down = None
+    for k in range(3):
+        up_send = own(3 + z - k)
+        down_send = own(z - 3 + k)
+        if k > 0:
+            up_send = up_send + up.astype(F32)
+            down_send = down_send + down.astype(F32)
+        lower = [n for n in range(8) if n // 2 <= min(k, 2)]
+        upper = [n for n in range(8) if 3 - n // 2 <= min(k, 2)]
+        up = lax.ppermute(up_send.astype(BF), "tile", [(n, n + 2) for n in lower])
+        down = lax.ppermute(down_send.astype(BF), "tile", [(n, n - 2) for n in upper])
+    total = (own(z) + up.astype(F32) + down.astype(F32)).astype(BF)
+
+    body = total[:, : 5 * HALF].reshape(2, 5, HALF, S)
+    row128 = total[:, 5 * HALF : 5 * HALF + 3]
+    extra = jnp.stack([row128[:, 0], row128[:, 0], row128[:, 0], row128[:, 1], row128[:, 2]], axis=1)[:, :, None]
+    later = jnp.concatenate([body[:, :, 1:], extra], axis=2)
+    shifted = jnp.concatenate([later[:, :1], body[:, 1:3], later[:, 3:]], axis=1)
+    deal = jnp.stack([body[:, :, :64], body[:, :, 64:], shifted[:, :, 64:], shifted[:, :, :64]])
+    got = lax.all_to_all(deal, "segment", split_axis=0, concat_axis=0, tiled=True)
+
+    weight_sum = jnp.sum(seeing, axis=0)
+    theta = pick(offset[..., 1], tile, 0).astype(F32) * (2.0 * jnp.pi / S)
+    scal = jnp.stack([1.0 / weight_sum, jnp.cos(theta), jnp.sin(theta)], axis=1).reshape(-1)
+    plain = seg < 2
+    v = np.arange(S)
+    eye = np.eye(S, dtype=np.float32)
+    flip = jnp.where(plain, eye, eye[(-v) % S]).astype(BF)
+    rot = jnp.where(plain, eye, eye[S - 1 - v]).astype(BF)
+    small = np.eye(64, dtype=np.float32)
+    lines = jnp.where(plain, small, small[::-1]).astype(BF)
+    return finish(scal, got, flip, rot, lines)
 
 
 def ramp_rows(taper, size):
@@ -113,8 +399,13 @@
 
 def solution(mesh):
     placed = (P(("segment", "tile"), None, None), P(), P(), P(None, "tile"), P(), P())
+    fits = mesh.shape["segment"] == 4 and mesh.shape["tile"] == 8
+
+    def run(raw_frames, *rest):
+        return (planes if fits and raw_frames.shape == (1, 1280, 1280) else local)(raw_frames, *rest)
+
     return jax.shard_map(
-        local,
+        run,
         mesh=mesh,
         in_specs=placed,
         out_specs=(P("tile", "segment", None), P("tile", None, "segment", None)),

time: 752 us -> 247 us (0.33)
  local copies, waits for them, and re-layouts: 309 us -> 17.9 us
  waiting for transfers between devices: 251 us -> 123 us
  other arithmetic: 109 us -> 19 us
  matrix products: 56.3 us -> 0 us
  Pallas kernels: 0 us -> 52.3 us
  starting transfers between devices: 6.43 us -> 33.4 us
  between operations: 14.1 us -> 0.94 us
    gather x192 -> x0, local copies, waits for them, and re-layouts: 242 us -> none
    all_to_all x1 -> x3, waiting for transfers between devices: 182 us -> 63.9 us  [the longest x1 52.4 us: planes(): lax.all_to_all(send, 'segment', split_axis=0, concat_axis=0, tiled=True)]
    reduce_scatter x2 -> x0, waiting for transfers between devices: 68.7 us -> none  [the longest x1 53.6 us: local(): lax.psum_scatter(cross_sum.astype(jnp.bfloat16), 'segment', scatter_dimen...]
    ppermute x0 -> x7, waiting for transfers between devices: none -> 59.1 us  [the longest x3 35.3 us: planes(): up = lax.ppermute(up_send.astype(BF), 'tile', [(n, n + 2) for n in lower])]
    dot_general x3 -> x0, matrix products: 56.3 us -> none  [the longest x1 22.3 us: second_pass(): jnp.einsum('ux,fsxk->fsuk', sine, half, preferred_element_type=jnp.float32)]
    pallas_call x0 -> x2, Pallas kernels: none -> 52.3 us  [the longest x1 46.7 us: spectra(): pl.pallas_call(lambda *refs: spectra_body(n_frames, *refs), out_shape=(ou...]
    slice x8 -> x6, local copies, waits for them, and re-layouts: 50.5 us -> 3.1 us  [the longest x1 2.87 us: planes(): send = jnp.stack([raw_frames[0, :, S * d:S * d + 2 * S] for d in range(4)])]
    reduce_sum x3 -> x1, other arithmetic: 46.9 us -> 0.12 us  [planes(): weight_sum = jnp.sum(seeing, axis=0)]
  transfers between devices with their start and end apart: 3 -> 10, of which waited for: 3 -> 7; matrix products, arithmetic and copies ran while one was open for 2% -> 8% of each run, Pallas kernels for 0% -> 0%
where the time goes in v1:
time: 247 us
  waiting for transfers between devices  123 us (50%)
  Pallas kernels  52.3 us (21%)
  starting transfers between devices  33.4 us (14%)
  other arithmetic  19 us (8%)
  local copies, waits for them, and re-layouts  17.9 us (7%)
    all_to_all x1, waiting for transfers between devices, planes(): lax.all_to_all(send, 'segment', split_axis=0, concat_axis=0, tiled=True)  52.4 us
    pallas_call x1, Pallas kernels, spectra(): pl.pallas_call(lambda *refs: spectra_body(n_frames, *refs), out_shape=(ou...  46.7 us
    ppermute x3, waiting for transfers between devices, planes(): up = lax.ppermute(up_send.astype(BF), 'tile', [(n, n + 2) for n in lower])  35.3 us
    ppermute x3, waiting for transfers between devices, planes(): lax.ppermute(down_send.astype(BF), 'tile', [(n, n - 2) for n in upper])  18.6 us
    ppermute x3, starting transfers between devices, planes(): up = lax.ppermute(up_send.astype(BF), 'tile', [(n, n + 2) for n in lower])  13.8 us
    all_to_all x1, waiting for transfers between devices, planes(): lax.all_to_all(deal, 'segment', split_axis=0, concat_axis=0, tiled=True)  11.6 us
    convert_element_type x3, other arithmetic, planes(): up = lax.ppermute(up_send.astype(BF), 'tile', [(n, n + 2) for n in lower])  8.68 us
    all_to_all x1, starting transfers between devices, planes(): lax.all_to_all(by_tile, 'tile', split_axis=0, concat_axis=0, tiled=True)  6.35 us
  transfers between devices with their start and end apart: 10, of which 7 were waited for; matrix products, arithmetic and copies ran while one was open for 8% of the time, Pallas kernels for 0%

profile of v1, /device:TPU:0, one launch (start us, length us, event | category | flops | bytes accessed | tf_op | source)
XLA Modules:
  0.0 246.5 jit_solution(16279756789734157078)
XLA Ops:
  0.6 0.8 reshape.372
  2.1 6.4 %all-to-all-start = ((f32[8,4,8]{2,1,0:T(4,128)}), f32[8,4,8]{2,1,0:T(4,128)S(1)}, u32[]{:S(2)}, u32[]{:S(2)}) async-start(f32[8,4,8]{2,1,0:T(4,128)} %copy.49), calls=%async_computation | async-start | bytes 32768 | tf_op jit(solution)/shard_map/all_to_all | solution.py:232
  8.4 2.9 %fusion.31 = (bf16[1,1280,512]{2,1,0:T(8,128)(2,1)S(1)}, bf16[1,1280,512]{2,1,0:T(8,128)(2,1)S(1)}, bf16[1,1280,512]{2,1,0:T(8,128)(2,1)S(1)}, bf16[1,1280,512]{2,1,0:T(8,128)(2,1)S(1)}) fusion(bf16[1,1280,1280]{2,1,0:T(8,128)(2,1)} %param.13), kind=kLoop, calls=%fused_computation.79 | loop fusion | bytes 10485760 | tf_op jit(solution)/shard_map/slice | solution.py:228
  11.3 3.0 %pad_maximum_fusion = bf16[4,1280,512]{2,1,0:T(8,128)(2,1)} fusion(bf16[1,1280,512]{2,1,0:T(8,128)(2,1)S(1)} %get-tuple-element.12, bf16[1,1280,512]{2,1,0:T(8,128)(2,1)S(1)} %get-tuple-element.13, bf16[1,1280,512]{2,1,0:T(8,128)(2,1)S(1)} %get-tuple-element.11, bf16[1,1280,512]{2,1,0:T(8,128)(2,1)S(1)} %get-tuple-element.10), kind=kLoop, calls=%fused_computation | loop fusion | flops 7864320 | bytes 10485760 | tf_op jit(solution)/shard_map/stack | solution.py:228
  14.3 5.2 %all-to-all-start.1 = ((bf16[4,1280,512]{2,1,0:T(8,128)(2,1)}), bf16[4,1280,512]{2,1,0:T(8,128)(2,1)}, u32[]{:S(2)}, u32[]{:S(2)}) async-start(bf16[4,1280,512]{2,1,0:T(8,128)(2,1)} %pad_maximum_fusion), calls=%async_computation.1 | async-start | bytes 10485760 | tf_op jit(solution)/shard_map/all_to_all | solution.py:229
  22.3 3.5 %constant_dynamic-slice_fusion.2 = (bf16[1280,512]{1,0:T(8,128)(2,1)}, bf16[1280,512]{1,0:T(8,128)(2,1)}) fusion(bf16[1280,1280]{1,0:T(8,128)(2,1)} %param.15, s32[]{:T(128)S(6)} %select_n.144, bf16[1280,1280]{1,0:T(8,128)(2,1)} %param.14), kind=kLoop, calls=%fused_computation.57 | loop fusion | bytes 5242884 | tf_op jit(solution)/shard_map/dynamic_slice | solution.py:252
  26.7 52.4 %all-to-all-done.1.refs_2_.refs_3_ = bf16[4,1280,512]{2,1,0:T(8,128)(2,1)} async-done(((bf16[4,1280,512]{2,1,0:T(8,128)(2,1)}), bf16[4,1280,512]{2,1,0:T(8,128)(2,1)}, u32[]{:S(2)}, u32[]{:S(2)}) %all-to-all-start.1) | async-done | bytes 5242912 | tf_op jit(solution)/shard_map/all_to_all | solution.py:229
  79.1 1.9 broadcast_in_dim.59.refs_8_
  82.4 46.7 %spectra.1 = (bf16[4,2,656,256]{3,2,1,0:T(8,128)(2,1)}, bf16[4,2,656,256]{3,2,1,0:T(8,128)(2,1)}) custom-call(s32[16]{0:T(128)} %reshape.371.refs_0_, f32[64]{0:T(128)} %reshape.374.refs_1_, bf16[4,1280,512]{2,1,0:T(8,128)(2,1)} %all-to-all-done.1.refs_2_.refs_3_, bf16[4,1280,512]{2,1,0:T(8,128)(2,1)} %all-to-all-done.1.refs_2_.refs_3_, ...), custom_call_target="tpu_custom_call" | custom-call | flops 16000000000 | bytes 20000000 | tf_op jit(solution)/shard_map/spectra/pallas_call | solution.py:144
  129.1 5.2 %collective-permute-done = bf16[4,2,656,256]{3,2,1,0:T(8,128)(2,1)S(1)} collective-permute-done((bf16[4,2,656,256]{3,2,1,0:T(8,128)(2,1)}, bf16[4,2,656,256]{3,2,1,0:T(8,128)(2,1)S(1)}, u32[]{:S(2)}, u32[]{:S(2)}) %collective-permute-start) | collective-permute-done | bytes 2687008 | tf_op jit(solution)/shard_map/ppermute | solution.py:257
  134.3 1.5 copy-done.1
  135.8 3.0 %fusion.10 = (bf16[2,656,256]{2,1,0:T(8,128)(2,1)}, bf16[2,656,256]{2,1,0:T(8,128)(2,1)S(1)}) fusion(bf16[4,2,656,256]{3,2,1,0:T(8,128)(2,1)} %copy-done.1, s32[]{:T(128)S(6)} %min.25, bf16[4,2,656,256]{3,2,1,0:T(8,128)(2,1)} %get-tuple-element.4, s32[]{:T(128)S(6)} %min.28), kind=kLoop, calls=%fused_computation.21 | loop fusion | flops 2686976 | bytes 4030472 | tf_op jit(solution)/shard_map/convert_element_type | solution.py:272
  138.8 4.4 %collective-permute-start.1 = (bf16[2,656,256]{2,1,0:T(8,128)(2,1)}, bf16[2,656,256]{2,1,0:T(8,128)(2,1)}, u32[]{:S(2)}, u32[]{:S(2)}) collective-permute-start(bf16[2,656,256]{2,1,0:T(8,128)(2,1)} %get-tuple-element.8), channel_id=1, source_target_pairs={{0,2},{1,3},{8,10},{9,11},{16,18},{17,19},{24,26},{25,27}} | collective-permute-start | bytes 2015240 | tf_op jit(solution)/shard_map/ppermute | solution.py:272
  143.2 1.5 collective-permute-start.4
  144.7 12.6 %collective-permute-done.1 = bf16[2,656,256]{2,1,0:T(8,128)(2,1)} collective-permute-done((bf16[2,656,256]{2,1,0:T(8,128)(2,1)}, bf16[2,656,256]{2,1,0:T(8,128)(2,1)}, u32[]{:S(2)}, u32[]{:S(2)}) %collective-permute-start.1) | collective-permute-done | bytes 671776 | tf_op jit(solution)/shard_map/ppermute | solution.py:272
  157.3 2.4 fusion.2
  159.7 5.2 %collective-permute-start.2 = (bf16[2,656,256]{2,1,0:T(8,128)(2,1)}, bf16[2,656,256]{2,1,0:T(8,128)(2,1)}, u32[]{:S(2)}, u32[]{:S(2)}) collective-permute-start(bf16[2,656,256]{2,1,0:T(8,128)(2,1)} %fusion.2), channel_id=1, source_target_pairs={{0,2},{1,3},{2,4},{3,5},{8,10},{9,11},{10,12},{11,13},{16,18},{17,... | collective-permute-start | bytes 2015240 | tf_op jit(solution)/shard_map/ppermute | solution.py:272
  164.9 13.2 %collective-permute-done.2 = bf16[2,656,256]{2,1,0:T(8,128)(2,1)} collective-permute-done((bf16[2,656,256]{2,1,0:T(8,128)(2,1)}, bf16[2,656,256]{2,1,0:T(8,128)(2,1)}, u32[]{:S(2)}, u32[]{:S(2)}) %collective-permute-start.2) | collective-permute-done | bytes 671776 | tf_op jit(solution)/shard_map/ppermute | solution.py:272
  178.2 3.3 %fusion.3 = (bf16[2,656,256]{2,1,0:T(8,128)(2,1)}, bf16[2,656,256]{2,1,0:T(8,128)(2,1)}) fusion(bf16[2,656,256]{2,1,0:T(8,128)(2,1)} %collective-permute-done.2, bf16[4,2,656,256]{3,2,1,0:T(8,128)(2,1)} %copy-done.1, s32[]{:T(128)S(6)} %min.23, bf16[4,2,656,256]{3,2,1,0:T(8,128)(2,1)S(1)} %copy-done, bf16[2,656,256]{2,1,0:T(8,128)(2,1)} %collective-permute-done.4, ...), kind=kLoop, calls=%fused_computation.8 | loop fusion | flops 4030464 | bytes 5373960 | tf_op jit(solution)/shard_map/convert_element_type | solution.py:272
  181.4 1.5 collective-permute-start.5
  182.9 4.2 %collective-permute-start.3 = (bf16[2,656,256]{2,1,0:T(8,128)(2,1)}, bf16[2,656,256]{2,1,0:T(8,128)(2,1)S(1)}, u32[]{:S(2)}, u32[]{:S(2)}) collective-permute-start(bf16[2,656,256]{2,1,0:T(8,128)(2,1)} %get-tuple-element.6), channel_id=1, source_target_pairs={{0,2},{1,3},{2,4},{3,5},{4,6},{5,7},{8,10},{9,11},{10,12},{11,13},... | collective-permute-start | bytes 2015240 | tf_op jit(solution)/shard_map/ppermute | solution.py:272
  187.2 2.4 fusion.1
  189.6 1.3 collective-permute-start.6
  190.9 9.5 %collective-permute-done.3 = bf16[2,656,256]{2,1,0:T(8,128)(2,1)S(1)} collective-permute-done((bf16[2,656,256]{2,1,0:T(8,128)(2,1)}, bf16[2,656,256]{2,1,0:T(8,128)(2,1)S(1)}, u32[]{:S(2)}, u32[]{:S(2)}) %collective-permute-start.3) | collective-permute-done | bytes 671776 | tf_op jit(solution)/shard_map/ppermute | solution.py:272
  200.4 18.6 %collective-permute-done.6 = bf16[2,656,256]{2,1,0:T(8,128)(2,1)} collective-permute-done((bf16[2,656,256]{2,1,0:T(8,128)(2,1)}, bf16[2,656,256]{2,1,0:T(8,128)(2,1)}, u32[]{:S(2)}, u32[]{:S(2)}) %collective-permute-start.6) | collective-permute-done | bytes 671776 | tf_op jit(solution)/shard_map/ppermute | solution.py:273
  218.9 1.6 fusion.5
  221.0 1.2 pad_maximum_fusion.1
  222.3 3.7 %all-to-all-start.2 = ((bf16[4,2,5,64,256]{4,3,2,1,0:T(8,128)(2,1)}), bf16[4,2,5,64,256]{4,3,2,1,0:T(8,128)(2,1)S(1)}, u32[]{:S(2)}, u32[]{:S(2)}) async-start(bf16[4,2,5,64,256]{4,3,2,1,0:T(8,128)(2,1)} %pad_maximum_fusion.1), calls=%async_computation.2 | async-start | bytes 2621440 | tf_op jit(solution)/shard_map/all_to_all | solution.py:282
  227.6 0.7 select_convert_fusion
  228.3 11.6 %all-to-all-done.2.x = bf16[4,2,5,64,256]{4,3,2,1,0:T(8,128)(2,1)S(1)} async-done(((bf16[4,2,5,64,256]{4,3,2,1,0:T(8,128)(2,1)}), bf16[4,2,5,64,256]{4,3,2,1,0:T(8,128)(2,1)S(1)}, u32[]{:S(2)}, u32[]{:S(2)}) %all-to-all-start.2) | async-done | bytes 1310752 | tf_op jit(solution)/shard_map/all_to_all | solution.py:282
  239.8 1.1 copy-done.2
  240.9 5.6 %finish.1 = (f32[8,64,256]{2,1,0:T(8,128)}, f32[8,4,64,256]{3,2,1,0:T(8,128)}) custom-call(f32[24]{0:T(128)} %reshape.369.scal, bf16[4,2,5,64,256]{4,3,2,1,0:T(8,128)(2,1)} %copy-done.2, bf16[256,256]{1,0:T(8,128)(2,1)} %get-tuple-element.19.flip, bf16[256,256]{1,0:T(8,128)(2,1)} %get-tuple-element.18.rot, bf16[64,64]{1,0:T(8,128)(2,1)} %select_convert_fusion.2.lines), custom_call_target="tpu_custom_call" | custom-call | flops 400000000 | bytes 4000000 | tf_op jit(solution)/shard_map/finish/pallas_call | solution.py:193
  (78 shorter events, 7.8 us)
Async XLA Ops:
  2.1 12.2 %all-to-all-start = ((f32[8,4,8]{2,1,0:T(4,128)}), f32[8,4,8]{2,1,0:T(4,128)S(1)}, u32[]{:S(2)}, u32[]{:S(2)}) async-start(f32[8,4,8]{2,1,0:T(4,128)} %copy.49), calls=%async_computation | async-start | bytes 32768 | tf_op jit(solution)/shard_map/all_to_all | solution.py:232
  14.3 5.2 %copy-start.9 = (s32[64,2]{0,1:T(2,128)S(1)}, s32[64,2]{0,1:T(2,128)}, u32[]{:S(2)}) copy-start(s32[64,2]{0,1:T(2,128)} %param.17) | copy-start | bytes 1540
  14.3 6.5 %copy-start.10 = (s32[64]{0:T(128)S(1)}, s32[64]{0:T(128)}, u32[]{:S(2)}) copy-start(s32[64]{0:T(128)} %param.18) | copy-start | bytes 772
  14.3 64.8 %all-to-all-start.1 = ((bf16[4,1280,512]{2,1,0:T(8,128)(2,1)}), bf16[4,1280,512]{2,1,0:T(8,128)(2,1)}, u32[]{:S(2)}, u32[]{:S(2)}) async-start(bf16[4,1280,512]{2,1,0:T(8,128)(2,1)} %pad_maximum_fusion), calls=%async_computation.1 | async-start | bytes 10485760 | tf_op jit(solution)/shard_map/all_to_all | solution.py:229
  129.0 5.3 %collective-permute-start = (bf16[4,2,656,256]{3,2,1,0:T(8,128)(2,1)}, bf16[4,2,656,256]{3,2,1,0:T(8,128)(2,1)S(1)}, u32[]{:S(2)}, u32[]{:S(2)}) collective-permute-start(bf16[4,2,656,256]{3,2,1,0:T(8,128)(2,1)} %get-tuple-element.5), channel_id=1, source_target_pairs={{0,1},{1,0},{2,3},{3,2},{4,5},{5,4},{6,7},{7,6},{8,9},{9,8},{10,11... | collective-permute-start | bytes 8060936 | tf_op jit(solution)/shard_map/ppermute | solution.py:257
  134.3 1.5 copy-start.1
  135.8 21.5 %copy-start = (bf16[4,2,656,256]{3,2,1,0:T(8,128)(2,1)S(1)}, bf16[4,2,656,256]{3,2,1,0:T(8,128)(2,1)}, u32[]{:S(2)}) copy-start(bf16[4,2,656,256]{3,2,1,0:T(8,128)(2,1)} %get-tuple-element.4) | copy-start | bytes 8060932
  138.8 18.5 %collective-permute-start.1 = (bf16[2,656,256]{2,1,0:T(8,128)(2,1)}, bf16[2,656,256]{2,1,0:T(8,128)(2,1)}, u32[]{:S(2)}, u32[]{:S(2)}) collective-permute-start(bf16[2,656,256]{2,1,0:T(8,128)(2,1)} %get-tuple-element.8), channel_id=1, source_target_pairs={{0,2},{1,3},{8,10},{9,11},{16,18},{17,19},{24,26},{25,27}} | collective-permute-start | bytes 2015240 | tf_op jit(solution)/shard_map/ppermute | solution.py:272
  143.2 21.7 %collective-permute-start.4 = (bf16[2,656,256]{2,1,0:T(8,128)(2,1)S(1)}, bf16[2,656,256]{2,1,0:T(8,128)(2,1)}, u32[]{:S(2)}, u32[]{:S(2)}) collective-permute-start(bf16[2,656,256]{2,1,0:T(8,128)(2,1)S(1)} %get-tuple-element.9), channel_id=1, source_target_pairs={{6,4},{7,5},{14,12},{15,13},{22,20},{23,21},{30,28},{31,29}} | collective-permute-start | bytes 2015240 | tf_op jit(solution)/shard_map/ppermute | solution.py:273
  159.7 18.5 %collective-permute-start.2 = (bf16[2,656,256]{2,1,0:T(8,128)(2,1)}, bf16[2,656,256]{2,1,0:T(8,128)(2,1)}, u32[]{:S(2)}, u32[]{:S(2)}) collective-permute-start(bf16[2,656,256]{2,1,0:T(8,128)(2,1)} %fusion.2), channel_id=1, source_target_pairs={{0,2},{1,3},{2,4},{3,5},{8,10},{9,11},{10,12},{11,13},{16,18},{17,... | collective-permute-start | bytes 2015240 | tf_op jit(solution)/shard_map/ppermute | solution.py:272
  181.4 5.7 %collective-permute-start.5 = (bf16[2,656,256]{2,1,0:T(8,128)(2,1)}, bf16[2,656,256]{2,1,0:T(8,128)(2,1)}, u32[]{:S(2)}, u32[]{:S(2)}) collective-permute-start(bf16[2,656,256]{2,1,0:T(8,128)(2,1)} %get-tuple-element.7), channel_id=1, source_target_pairs={{4,2},{5,3},{6,4},{7,5},{12,10},{13,11},{14,12},{15,13},{20,18},{2... | collective-permute-start | bytes 2015240 | tf_op jit(solution)/shard_map/ppermute | solution.py:273
  182.9 17.4 %collective-permute-start.3 = (bf16[2,656,256]{2,1,0:T(8,128)(2,1)}, bf16[2,656,256]{2,1,0:T(8,128)(2,1)S(1)}, u32[]{:S(2)}, u32[]{:S(2)}) collective-permute-start(bf16[2,656,256]{2,1,0:T(8,128)(2,1)} %get-tuple-element.6), channel_id=1, source_target_pairs={{0,2},{1,3},{2,4},{3,5},{4,6},{5,7},{8,10},{9,11},{10,12},{11,13},... | collective-permute-start | bytes 2015240 | tf_op jit(solution)/shard_map/ppermute | solution.py:272
  189.6 29.4 %collective-permute-start.6 = (bf16[2,656,256]{2,1,0:T(8,128)(2,1)}, bf16[2,656,256]{2,1,0:T(8,128)(2,1)}, u32[]{:S(2)}, u32[]{:S(2)}) collective-permute-start(bf16[2,656,256]{2,1,0:T(8,128)(2,1)} %fusion.1), channel_id=1, source_target_pairs={{2,0},{3,1},{4,2},{5,3},{6,4},{7,5},{10,8},{11,9},{12,10},{13,11},... | collective-permute-start | bytes 2015240 | tf_op jit(solution)/shard_map/ppermute | solution.py:273
  222.3 3.7 %copy-start.8 = (f32[32,8]{0,1:T(8,128)S(1)}, f32[32,8]{0,1:T(8,128)}, u32[]{:S(2)}) copy-start(f32[32,8]{0,1:T(8,128)} %param.16) | copy-start | bytes 3076
  222.3 4.7 %copy-start.6 = (bf16[64,64]{1,0:T(8,128)(2,1)S(1)}, bf16[64,64]{1,0:T(8,128)(2,1)}, u32[]{:S(2)}) copy-start(bf16[64,64]{1,0:T(8,128)(2,1)} %constant.216) | copy-start | bytes 24580
  222.3 4.7 %copy-start.7 = (bf16[64,64]{1,0:T(8,128)(2,1)S(1)}, bf16[64,64]{1,0:T(8,128)(2,1)}, u32[]{:S(2)}) copy-start(bf16[64,64]{1,0:T(8,128)(2,1)} %constant.217) | copy-start | bytes 24580
  222.3 5.3 %copy-start.3 = (bf16[256,256]{1,0:T(8,128)(2,1)S(1)}, bf16[256,256]{1,0:T(8,128)(2,1)}, u32[]{:S(2)}) copy-start(bf16[256,256]{1,0:T(8,128)(2,1)} %constant.213) | copy-start | bytes 393220
  222.3 5.3 %copy-start.4 = (bf16[256,256]{1,0:T(8,128)(2,1)S(1)}, bf16[256,256]{1,0:T(8,128)(2,1)}, u32[]{:S(2)}) copy-start(bf16[256,256]{1,0:T(8,128)(2,1)} %constant.215) | copy-start | bytes 393220
  222.3 5.3 %copy-start.5 = (bf16[256,256]{1,0:T(8,128)(2,1)S(1)}, bf16[256,256]{1,0:T(8,128)(2,1)}, u32[]{:S(2)}) copy-start(bf16[256,256]{1,0:T(8,128)(2,1)} %constant.214) | copy-start | bytes 393220
  222.3 17.5 %all-to-all-start.2 = ((bf16[4,2,5,64,256]{4,3,2,1,0:T(8,128)(2,1)}), bf16[4,2,5,64,256]{4,3,2,1,0:T(8,128)(2,1)S(1)}, u32[]{:S(2)}, u32[]{:S(2)}) async-start(bf16[4,2,5,64,256]{4,3,2,1,0:T(8,128)(2,1)} %pad_maximum_fusion.1), calls=%async_computation.2 | async-start | bytes 2621440 | tf_op jit(solution)/shard_map/all_to_all | solution.py:282
  239.8 1.1 copy-start.2
